TPU v7x, 32 devices: a whole 2x2x4 slice. The times are simulated.
32 devices in a mesh: row: 4 (over y, core), col: 8 (over z, x).
Axes of the slice: x: 2, y: 2, z: 4, core: 2. Of those that a mesh axis runs over, the one named last changes fastest.
Arguments:
- points: bfloat16 [65536, 512], P(('row', 'col')), may hold values from -6 to 6
- factor: bfloat16 [65536, 2048], P(('row', 'col')), may hold values from -0.078125 to 0.078125
- targets: bfloat16 [65536, 256], P(('row', 'col')), may hold values from -6 to 6
- pivot_slots: int32 [32, 32], P(('row', 'col')), may hold values from 0 to 2047, as said below
- pivot_counts: int32 [32], replicated, may hold values from 1 to 32, 512 in all
Outputs:
- new_columns: bfloat16 [512, 65536], P(None, ('row', 'col'))
- residual_next: float32 [65536, 256], P(('row', 'col'))
Inputs may be any that keep to these rules, and one draw needn't show every extreme that they name: `pivot_slots`: each row holds 32 different local row numbers; row d's first pivot_counts[d] entries are device d's pivots, the rest are unused. `pivot_counts`: the counts sum to 512; one of them is 32.
All inputs are finite; a program needn't handle non-finite values.
Results may differ from a plain program's by a relative error of at most 0.0029.
Values may be sent and summed in bfloat16 or wider, within the bound.
No kernel may reach another device: no remote copies, remote signals or barrier semaphores. Data moves between devices by JAX's collectives and lax.ppermute only.
A program may use at most 128 MiB of HBM per device.

v0:
```python
import jax
import jax.numpy as jnp
from jax import lax
from jax.sharding import PartitionSpec as P

BLOCK = 512
sharpness = 1.0
ridge_shift = 0.01
damping = 1.0
epsilon = 1e-06


def normalize(points):
    values = points.astype(jnp.float32)
    factor_scale = lax.rsqrt(jnp.mean(values * values, axis=1, keepdims=True) + epsilon)
    return (values * factor_scale).astype(jnp.bfloat16)


def kernel(left_rows, right_rows, feature_width):
    cosine = (
        lax.dot_general(
            left_rows, right_rows, (((1,), (1,)), ((), ())), preferred_element_type=jnp.float32
        )
        / feature_width
    )
    return jnp.exp(sharpness * (cosine - 1.0))


def compact_index(pivot_counts, block_size):
    owners_count = pivot_counts.shape[0]
    run_ends = jnp.cumsum(pivot_counts)
    run_starts = run_ends - pivot_counts
    position = jnp.arange(block_size, dtype=jnp.int32)
    owners = jnp.sum((position[:, None] >= run_ends[None, :]).astype(jnp.int32), axis=1)
    onehot = (owners[:, None] == jnp.arange(owners_count, dtype=jnp.int32)[None, :]).astype(
        jnp.int32
    )
    first_row = jnp.sum(onehot * run_starts[None, :], axis=1)
    return (owners, position - first_row)


def block_factor(pivot_scaled, pivot_factor):
    intersection = lax.dot_general(
        pivot_factor, pivot_factor, (((1,), (1,)), ((), ())), preferred_element_type=jnp.float32
    )
    diag_shift = ridge_shift + jnp.max(jnp.sum(jnp.abs(intersection), axis=1))
    ridged = (
        kernel(pivot_scaled, pivot_scaled, pivot_scaled.shape[1])
        - intersection
        + diag_shift * jnp.eye(intersection.shape[0], dtype=jnp.float32)
    )
    return jnp.linalg.cholesky(ridged)


def on_device(points, factor, targets, pivot_slots, pivot_counts):
    scaled = normalize(points)
    local_slots = pivot_slots[0]
    slot_cap = pivot_slots.shape[1]
    own_scaled = jnp.take(scaled, local_slots, axis=0)
    own_factor = jnp.take(factor, local_slots, axis=0)
    inner_scaled, inner_factor = (
        lax.all_gather(own_scaled, "col", axis=0, tiled=True),
        lax.all_gather(own_factor, "col", axis=0, tiled=True),
    )
    padded_scaled, padded_factor = (
        lax.all_gather(inner_scaled, "row", axis=0, tiled=True),
        lax.all_gather(inner_factor, "row", axis=0, tiled=True),
    )
    owners, slot_index = compact_index(pivot_counts, BLOCK)
    row_index = owners * slot_cap + slot_index
    pivot_scaled = jnp.take(padded_scaled, row_index, axis=0)
    pivot_factor = jnp.take(padded_factor, row_index, axis=0)
    lower_factor = block_factor(pivot_scaled, pivot_factor)
    downdated = kernel(pivot_scaled, scaled, scaled.shape[1]) - lax.dot_general(
        pivot_factor, factor, (((1,), (1,)), ((), ())), preferred_element_type=jnp.float32
    )
    new_columns = lax.linalg.triangular_solve(
        lower_factor, downdated, left_side=True, lower=True
    ).astype(jnp.bfloat16)
    cross_terms = jnp.concatenate(
        [
            lax.dot_general(
                factor, targets, (((0,), (0,)), ((), ())), preferred_element_type=jnp.float32
            ),
            lax.dot_general(
                new_columns, targets, (((1,), (0,)), ((), ())), preferred_element_type=jnp.float32
            ),
        ],
        axis=0,
    )
    col_norms = jnp.concatenate(
        [
            jnp.sum(jnp.square(factor.astype(jnp.float32)), axis=0),
            jnp.sum(jnp.square(new_columns.astype(jnp.float32)), axis=1),
        ],
        axis=0,
    )
    cross_whole, norm_whole = lax.psum((cross_terms, col_norms), ("row", "col"))
    coefficients = (cross_whole / (norm_whole + damping)[:, None]).astype(jnp.bfloat16)
    held_count = factor.shape[1]
    fitted = jnp.dot(factor, coefficients[:held_count], preferred_element_type=jnp.float32)
    fitted = fitted + lax.dot_general(
        new_columns,
        coefficients[held_count:],
        (((0,), (0,)), ((), ())),
        preferred_element_type=jnp.float32,
    )
    residual_next = targets.astype(jnp.float32) - fitted
    return (new_columns, residual_next)


def solution(mesh):
    return jax.shard_map(
        on_device,
        mesh=mesh,
        in_specs=(
            P(("row", "col"), None),
            P(("row", "col"), None),
            P(("row", "col"), None),
            P(("row", "col"), None),
            P(),
        ),
        out_specs=(P(None, ("row", "col")), P(("row", "col"), None)),
        check_vma=False,
    )
```

profile of v0, /device:TPU:0, one launch (start us, length us, event | category | flops | bytes accessed | tf_op | source)
XLA Modules:
  0.0 457.6 jit_solution(8331831617520132772)
XLA Ops:
  8.5 5.2 %gather_fusion.2 = bf16[32,2048]{1,0:T(8,128)(2,1)S(1)} fusion(bf16[2048,2048]{1,0:T(8,128)(2,1)} %param.6, s32[1024]{0:T(1024)S(1)} %pad_clamp_fusion.1), kind=kCustom, calls=%fused_computation.2 | custom fusion | bytes 262272 | tf_op jit(solution)/shard_map/jit(_take)/gather | solution.py:60
  14.6 2.2 fusion
  18.0 35.1 %all_gather.12 = bf16[256,512]{1,0:T(8,128)(2,1)} all-gather(bf16[32,512]{1,0:T(8,128)(2,1)S(1)} %broadcast_select_fusion.7), channel_id=1, replica_groups=mesh['row'=4,'col'=8] {'col'}, dimensions={0}, use_global_device_ids=true | all-gather | bytes 294912 | tf_op jit(solution)/shard_map/all_gather | solution.py:62
  53.2 5.6 %all-gather.6.cloned.1.call-done = bf16[256,2048]{1,0:T(8,128)(2,1)} async-done(((bf16[32,2048]{1,0:T(8,128)(2,1)}), bf16[256,2048]{1,0:T(8,128)(2,1)}) %all-gather.6.cloned.1.call-update) | async-done | bytes 1048592 | tf_op jit(solution)/shard_map/all_gather | solution.py:63
  59.5 7.2 %fusion.51 = f32[2048,256]{1,0:T(8,128)} fusion(bf16[2048,2048]{1,0:T(8,128)(2,1)} %param.6, bf16[2048,256]{1,0:T(8,128)(2,1)S(1)} %copy-done.6), kind=kOutput, calls=%fused_computation.122 | convolution fusion | flops 2147483648 | bytes 11534336 | tf_op jit(solution)/shard_map/dot_general | solution.py:82
  66.7 9.0 %all-gather.4.cloned.1.call-done = bf16[1024,512]{1,0:T(8,128)(2,1)} async-done(((bf16[256,512]{1,0:T(8,128)(2,1)}), bf16[1024,512]{1,0:T(8,128)(2,1)}) %all-gather.4.cloned.1.call-update) | async-done | bytes 1048592 | tf_op jit(solution)/shard_map/all_gather | solution.py:66
  75.7 4.0 gather_fusion.1
  79.7 32.0 %all-gather.8.cloned.1.call-done = bf16[1024,2048]{1,0:T(8,128)(2,1)} async-done(((bf16[256,2048]{1,0:T(8,128)(2,1)}), bf16[1024,2048]{1,0:T(8,128)(2,1)}) %all-gather.8.cloned.1.call-update) | async-done | bytes 4194320 | tf_op jit(solution)/shard_map/all_gather | solution.py:67
  111.8 8.0 %gather_fusion.3 = bf16[512,2048]{1,0:T(8,128)(2,1)} fusion(bf16[1024,2048]{1,0:T(8,128)(2,1)} %all-gather.8.cloned.1.call-done, s32[1024]{0:T(1024)S(1)} %pad_clamp_fusion), kind=kCustom, calls=%fused_computation.3 | custom fusion | bytes 4196352 | tf_op jit(solution)/shard_map/jit(_take)/gather | solution.py:72
  119.7 3.7 abs_reduce_fusion
  123.5 9.9 %fusion.21 = f32[512,2048]{1,0:T(8,128)} fusion(bf16[2048,2048]{1,0:T(8,128)(2,1)} %param.6, bf16[512,2048]{1,0:T(8,128)(2,1)S(1)} %copy-done.4, pred[512]{0:T(512)(128)(4,1)S(1)} %compare_and_fusion.1), kind=kOutput, calls=%fused_computation.51 | convolution fusion | flops 4296015872 | bytes 14680576 | tf_op jit(solution)/shard_map/dot_general | solution.py:74
  133.3 1.3 copy.20
  134.6 2.1 fusion.17
  136.8 1.3 copy.21
  139.3 1.4 add_multiply_fusion
  141.8 11.7 %cholesky.103 = f32[128,128]{1,0:T(8,128)S(1)} custom-call(f32[128,128]{1,0:T(8,128)S(1)} %cholesky.263), custom_call_target="Cholesky" | custom-call | tf_op jit(solution)/shard_map/jit(cholesky)/cholesky | solution.py:52
  153.7 9.8 %custom-call.30 = f32[1,128,128]{1,2,0:T(8,128)S(1)} custom-call(f32[1,128,128]{2,1,0:T(8,128)S(1)} %get-tuple-element.37), custom_call_target="InvertDiagBlocksLowerTriangular" | custom-call | tf_op jit(solution)/shard_map/jit(cholesky)/cholesky | solution.py:52
  163.5 1.2 constant_dynamic-update-slice_fusion.3
  164.7 1.3 convolution_subtract_fusion.2
  166.0 11.7 %cholesky.215 = f32[128,128]{1,0:T(8,128)S(1)} custom-call(f32[128,128]{1,0:T(8,128)S(1)} %cholesky.267), custom_call_target="Cholesky" | custom-call | tf_op jit(solution)/shard_map/jit(cholesky)/cholesky | solution.py:52
  177.8 10.2 %custom-call.31 = f32[1,128,128]{1,2,0:T(8,128)S(1)} custom-call(f32[1,128,128]{2,1,0:T(8,128)S(1)} %get-tuple-element.34), custom_call_target="InvertDiagBlocksLowerTriangular" | custom-call | tf_op jit(solution)/shard_map/jit(cholesky)/cholesky | solution.py:52
  188.3 1.3 convolution_subtract_fusion.3
  189.6 11.7 %cholesky.236 = f32[128,128]{1,0:T(8,128)S(1)} custom-call(f32[128,128]{1,0:T(8,128)S(1)} %cholesky.272), custom_call_target="Cholesky" | custom-call | tf_op jit(solution)/shard_map/jit(cholesky)/cholesky | solution.py:52
  202.0 9.8 %custom-call.32 = f32[1,128,128]{1,2,0:T(8,128)S(1)} custom-call(f32[1,128,128]{2,1,0:T(8,128)S(1)} %get-tuple-element.31), custom_call_target="InvertDiagBlocksLowerTriangular" | custom-call | tf_op jit(solution)/shard_map/jit(cholesky)/cholesky | solution.py:52
  212.0 1.2 convolution_subtract_fusion.4
  213.2 11.8 %cholesky.253 = f32[128,128]{1,0:T(8,128)S(1)} custom-call(f32[128,128]{1,0:T(8,128)S(1)} %convolution_subtract_fusion.4), custom_call_target="Cholesky" | custom-call | tf_op jit(solution)/shard_map/jit(cholesky)/cholesky | solution.py:52
  228.8 1.1 select_select_fusion
  229.9 13.6 %while.1 = (s32[]{:T(128)}, f32[512,512]{1,0:T(8,128)}, s32[4,2]{0,1:T(2,128)S(1)}, f32[4,128,128]{2,1,0:T(8,128)}, s32[]{:T(128)}) while((s32[]{:T(128)}, f32[512,512]{1,0:T(8,128)}, s32[4,2]{0,1:T(2,128)S(1)}, f32[4,128,128]{2,1,0:T(8,128)}, s32[]{:T(128)}) %tuple.39), condition=%wide.while_cond, body=%wide.while_body.sunk | while | flops 2 | bytes 132705 | solution.py:77
  230.6 2.8 bitcast_dynamic-update-slice_fusion.2
  234.0 2.8 bitcast_dynamic-update-slice_fusion.2
  237.4 2.8 bitcast_dynamic-update-slice_fusion.2
  240.8 2.7 bitcast_dynamic-update-slice_fusion.2
  243.6 40.1 %custom-call.33 = f32[4,128,128]{1,2,0:T(8,128)S(1)} custom-call(f32[4,128,128]{2,1,0:T(8,128)} %get-tuple-element.9), custom_call_target="InvertDiagBlocksLowerTriangular" | custom-call | tf_op jit(solution)/shard_map/triangular_solve | solution.py:77
  283.7 3.7 exponential_subtract_fusion
  287.4 1.1 fusion.50
  288.5 1.9 convolution_subtract_fusion.1
  291.4 2.2 convolution_subtract_fusion
  293.6 1.0 fusion.48
  294.7 3.0 fusion.9
  297.7 1.1 convolution_convert_fusion
  299.4 1.3 copy-done
  301.7 1.7 pad_maximum_fusion
  304.3 5.1 %multiply_reduce_fusion = f32[2048]{0:T(1024)S(1)} fusion(bf16[2048,2048]{1,0:T(8,128)(2,1)} %param.6), kind=kLoop, calls=%fused_computation.6 | loop fusion | flops 12580864 | bytes 8396800 | tf_op jit(solution)/shard_map/reduce_sum | solution.py:93
  309.4 39.6 %psum.15 = f32[2560]{0:T(1024)S(1)} all-reduce(f32[2560]{0:T(1024)S(1)} %pad_maximum_fusion.2), channel_id=1, replica_groups=mesh['row'=4,'col'=8] {'row','col'}, use_global_device_ids=true, to_apply=%region_17.18 | all-reduce | flops 2560 | bytes 20480 | tf_op jit(solution)/shard_map/psum | solution.py:98
  349.0 91.1 %all-reduce.3.cloned.1.call-done = f32[2560,256]{1,0:T(8,128)} async-done(((f32[2560,256]{1,0:T(8,128)}), f32[2560,256]{1,0:T(8,128)}) %all-reduce.3.cloned.1.call-update) | async-done | bytes 2621456 | tf_op jit(solution)/shard_map/psum | solution.py:98
  440.1 2.1 divide_convert_fusion
  442.3 5.9 %convolution_bitcast_fusion = f32[2048,256]{0,1:T(8,128)S(1)} fusion(bf16[2048,2048]{1,0:T(8,128)(2,1)} %param.6, bf16[2560,256]{1,0:T(8,128)(2,1)S(1)} %divide_convert_fusion), kind=kOutput, calls=%fused_computation.21 | convolution fusion | flops 2147483648 | bytes 11534336 | tf_op jit(solution)/shard_map/dot_general | solution.py:101
  449.0 1.8 copy.24
  (75 shorter events, 15.2 us)
Async XLA Ops:
  7.2 51.6 %all-gather.6.cloned.1.call-start = ((), (), s32[]{:S(2)}) async-start(), calls=%async_computation.1 | async-start | bytes 1179648 | tf_op jit(solution)/shard_map/all_gather | solution.py:63
  14.5 61.2 %all-gather.4.cloned.1.call-start = ((), (), s32[]{:S(2)}) async-start(), calls=%async_computation | async-start | bytes 1310720 | tf_op jit(solution)/shard_map/all_gather | solution.py:66
  14.6 2.3 copy-start.2
  16.8 42.1 %copy-start.8 = (s32[32]{0:T(128)S(1)}, s32[32]{0:T(128)}, u32[]{:S(2)}) copy-start(s32[32]{0:T(128)} %param.9) | copy-start | bytes 388
  16.9 42.7 %copy-start.6 = (bf16[2048,256]{1,0:T(8,128)(2,1)S(1)}, bf16[2048,256]{1,0:T(8,128)(2,1)}, u32[]{:S(2)}) copy-start(bf16[2048,256]{1,0:T(8,128)(2,1)} %param.7) | copy-start | bytes 3145732
  53.1 58.6 %all-gather.8.cloned.1.call-start = ((), (), s32[]{:S(2)}) async-start(), calls=%async_computation.2 | async-start | bytes 5242880 | tf_op jit(solution)/shard_map/all_gather | solution.py:67
  58.8 381.4 %all-reduce.3.cloned.1.call-start = ((), (), s32[]{:S(2)}) async-start(), calls=%async_computation.3 | async-start | bytes 5242880 | tf_op jit(solution)/shard_map/psum | solution.py:98
  119.7 3.8 copy-start.4
  140.8 1.0 copy-start.3
  297.7 3.0 copy-start.7
  299.4 1.3 copy-start
  299.4 2.3 copy-start.5
  442.3 5.9 %copy-start.1 = (bf16[512,2048]{1,0:T(8,128)(2,1)S(1)}, bf16[512,2048]{1,0:T(8,128)(2,1)}, u32[]{:S(2)}) copy-start(bf16[512,2048]{1,0:T(8,128)(2,1)} %copy-done) | copy-start | bytes 6291460
Sparse Core Ops, SparseCore 0:
  14.7 44.0 all-gather.5
  60.3 15.3 all-gather.3
  77.3 34.4 all-gather.7
  303.6 136.5 all-reduce.2
where the time goes:
time: 461 us; the launch traced here: 458 us
  waiting for transfers between devices  138 us (30%)
  other arithmetic  137 us (30%)
  blocking collectives  74.7 us (16%)
  matrix products  50.8 us (11%)
  local copies, waits for them, and re-layouts  39.5 us (9%)
  between operations  17.5 us (4%)
    psum x1, waiting for transfers between devices, on_device(): cross_whole, norm_whole = lax.psum((cross_terms, col_norms), ('row', 'col'))  91.1 us
    another operation x14, other arithmetic, block_factor(): return jnp.linalg.cholesky(ridged)  78.9 us
    another operation x3, other arithmetic, on_device(): lax.linalg.triangular_solve(lower_factor, downdated, left_side=True, lowe...  41.2 us
    psum x1, blocking collectives, on_device(): cross_whole, norm_whole = lax.psum((cross_terms, col_norms), ('row', 'col'))  39.6 us
    all_gather x1, blocking collectives, on_device(): lax.all_gather(own_scaled, 'col', axis=0, tiled=True)  35.1 us
    all_gather x1, waiting for transfers between devices, on_device(): lax.all_gather(inner_factor, 'row', axis=0, tiled=True)  32 us
    another operation x13, local copies, waits for them, and re-layouts  13.7 us
    another operation x7, matrix products, on_device(): lax.linalg.triangular_solve(lower_factor, downdated, left_side=True, lowe...  11.3 us
  transfers between devices with their start and end apart: 4, of which 4 were waited for; matrix products, arithmetic and copies ran while one was open for 5% of the time, Pallas kernels for 0%

commit v1 on v0

--- a/solution.py
+++ b/solution.py
@@ -95,7 +95,7 @@
         ],
         axis=0,
     )
-    cross_whole, norm_whole = lax.psum((cross_terms, col_norms), ("row", "col"))
+    cross_whole, norm_whole = lax.psum(lax.psum((cross_terms, col_norms), "row"), "col")
     coefficients = (cross_whole / (norm_whole + damping)[:, None]).astype(jnp.bfloat16)
     held_count = factor.shape[1]
     fitted = jnp.dot(factor, coefficients[:held_count], preferred_element_type=jnp.float32)

time: 461 us -> 505 us (1.095)
  waiting for transfers between devices: 138 us -> 172 us
  blocking collectives: 74.7 us -> 84.1 us
    psum x1 -> x2, waiting for transfers between devices: 91.1 us -> 125 us  [the longest x1 65.2 us: on_device(): lax.psum(lax.psum((cross_terms, col_norms), 'row'), 'col')]
    psum x1 -> x2, blocking collectives: 39.6 us -> 49 us  [the longest x1 38.5 us: on_device(): lax.psum(lax.psum((cross_terms, col_norms), 'row'), 'col')]
  transfers between devices with their start and end apart: 4 -> 5, of which waited for: 4 -> 5; matrix products, arithmetic and copies ran while one was open for 5% -> 4% of each run, Pallas kernels for 0% -> 0%
where the time goes in v1:
time: 505 us; the launch traced here: 501 us
  waiting for transfers between devices  172 us (34%)
  other arithmetic  137 us (27%)
  blocking collectives  84.1 us (17%)
  matrix products  50.8 us (10%)
  local copies, waits for them, and re-layouts  39.5 us (8%)
  between operations  17.5 us (3%)
    another operation x14, other arithmetic, block_factor(): return jnp.linalg.cholesky(ridged)  78.9 us
    psum x1, waiting for transfers between devices, on_device(): lax.psum(lax.psum((cross_terms, col_norms), 'row'), 'col')  65.2 us
    psum x1, waiting for transfers between devices, on_device(): lax.psum((cross_terms, col_norms), 'row')  60 us
    another operation x3, other arithmetic, on_device(): lax.linalg.triangular_solve(lower_factor, downdated, left_side=True, lowe...  41.2 us
    psum x1, blocking collectives, on_device(): lax.psum(lax.psum((cross_terms, col_norms), 'row'), 'col')  38.5 us
    all_gather x1, blocking collectives, on_device(): lax.all_gather(own_scaled, 'col', axis=0, tiled=True)  35.1 us
    all_gather x1, waiting for transfers between devices, on_device(): lax.all_gather(inner_factor, 'row', axis=0, tiled=True)  32 us
    another operation x13, local copies, waits for them, and re-layouts  13.7 us
  transfers between devices with their start and end apart: 5, of which 5 were waited for; matrix products, arithmetic and copies ran while one was open for 4% of the time, Pallas kernels for 0%

profile of v1, /device:TPU:0, one launch (start us, length us, event | category | flops | bytes accessed | tf_op | source)
XLA Modules:
  0.0 501.2 jit_solution(12826020302805920670)
XLA Ops:
  8.5 5.2 %gather_fusion.2 = bf16[32,2048]{1,0:T(8,128)(2,1)S(1)} fusion(bf16[2048,2048]{1,0:T(8,128)(2,1)} %param.6, s32[1024]{0:T(1024)S(1)} %pad_clamp_fusion.1), kind=kCustom, calls=%fused_computation.2 | custom fusion | bytes 262272 | tf_op jit(solution)/shard_map/jit(_take)/gather | solution.py:60
  14.6 2.2 fusion
  18.0 35.1 %all_gather.12 = bf16[256,512]{1,0:T(8,128)(2,1)} all-gather(bf16[32,512]{1,0:T(8,128)(2,1)S(1)} %broadcast_select_fusion.7), channel_id=1, replica_groups=mesh['row'=4,'col'=8] {'col'}, dimensions={0}, use_global_device_ids=true | all-gather | bytes 294912 | tf_op jit(solution)/shard_map/all_gather | solution.py:62
  53.2 5.6 %all-gather.6.cloned.1.call-done = bf16[256,2048]{1,0:T(8,128)(2,1)} async-done(((bf16[32,2048]{1,0:T(8,128)(2,1)}), bf16[256,2048]{1,0:T(8,128)(2,1)}) %all-gather.6.cloned.1.call-update) | async-done | bytes 1048592 | tf_op jit(solution)/shard_map/all_gather | solution.py:63
  59.5 7.2 %fusion.51 = f32[2048,256]{1,0:T(8,128)} fusion(bf16[2048,2048]{1,0:T(8,128)(2,1)} %param.6, bf16[2048,256]{1,0:T(8,128)(2,1)S(1)} %copy-done.6), kind=kOutput, calls=%fused_computation.122 | convolution fusion | flops 2147483648 | bytes 11534336 | tf_op jit(solution)/shard_map/dot_general | solution.py:82
  66.7 9.0 %all-gather.4.cloned.1.call-done = bf16[1024,512]{1,0:T(8,128)(2,1)} async-done(((bf16[256,512]{1,0:T(8,128)(2,1)}), bf16[1024,512]{1,0:T(8,128)(2,1)}) %all-gather.4.cloned.1.call-update) | async-done | bytes 1048592 | tf_op jit(solution)/shard_map/all_gather | solution.py:66
  75.7 4.0 gather_fusion.1
  79.7 32.0 %all-gather.8.cloned.1.call-done = bf16[1024,2048]{1,0:T(8,128)(2,1)} async-done(((bf16[256,2048]{1,0:T(8,128)(2,1)}), bf16[1024,2048]{1,0:T(8,128)(2,1)}) %all-gather.8.cloned.1.call-update) | async-done | bytes 4194320 | tf_op jit(solution)/shard_map/all_gather | solution.py:67
  111.8 8.0 %gather_fusion.3 = bf16[512,2048]{1,0:T(8,128)(2,1)} fusion(bf16[1024,2048]{1,0:T(8,128)(2,1)} %all-gather.8.cloned.1.call-done, s32[1024]{0:T(1024)S(1)} %pad_clamp_fusion), kind=kCustom, calls=%fused_computation.3 | custom fusion | bytes 4196352 | tf_op jit(solution)/shard_map/jit(_take)/gather | solution.py:72
  119.7 3.7 abs_reduce_fusion
  123.5 9.9 %fusion.21 = f32[512,2048]{1,0:T(8,128)} fusion(bf16[2048,2048]{1,0:T(8,128)(2,1)} %param.6, bf16[512,2048]{1,0:T(8,128)(2,1)S(1)} %copy-done.4, pred[512]{0:T(512)(128)(4,1)S(1)} %compare_and_fusion.1), kind=kOutput, calls=%fused_computation.51 | convolution fusion | flops 4296015872 | bytes 14680576 | tf_op jit(solution)/shard_map/dot_general | solution.py:74
  133.3 1.3 copy.20
  134.6 2.1 fusion.17
  136.8 1.3 copy.21
  139.3 1.4 add_multiply_fusion
  141.8 11.7 %cholesky.103 = f32[128,128]{1,0:T(8,128)S(1)} custom-call(f32[128,128]{1,0:T(8,128)S(1)} %cholesky.263), custom_call_target="Cholesky" | custom-call | tf_op jit(solution)/shard_map/jit(cholesky)/cholesky | solution.py:52
  153.7 9.8 %custom-call.30 = f32[1,128,128]{1,2,0:T(8,128)S(1)} custom-call(f32[1,128,128]{2,1,0:T(8,128)S(1)} %get-tuple-element.37), custom_call_target="InvertDiagBlocksLowerTriangular" | custom-call | tf_op jit(solution)/shard_map/jit(cholesky)/cholesky | solution.py:52
  163.5 1.2 constant_dynamic-update-slice_fusion.3
  164.7 1.3 convolution_subtract_fusion.2
  166.0 11.7 %cholesky.215 = f32[128,128]{1,0:T(8,128)S(1)} custom-call(f32[128,128]{1,0:T(8,128)S(1)} %cholesky.267), custom_call_target="Cholesky" | custom-call | tf_op jit(solution)/shard_map/jit(cholesky)/cholesky | solution.py:52
  177.8 10.2 %custom-call.31 = f32[1,128,128]{1,2,0:T(8,128)S(1)} custom-call(f32[1,128,128]{2,1,0:T(8,128)S(1)} %get-tuple-element.34), custom_call_target="InvertDiagBlocksLowerTriangular" | custom-call | tf_op jit(solution)/shard_map/jit(cholesky)/cholesky | solution.py:52
  188.3 1.3 convolution_subtract_fusion.3
  189.6 11.7 %cholesky.236 = f32[128,128]{1,0:T(8,128)S(1)} custom-call(f32[128,128]{1,0:T(8,128)S(1)} %cholesky.272), custom_call_target="Cholesky" | custom-call | tf_op jit(solution)/shard_map/jit(cholesky)/cholesky | solution.py:52
  202.0 9.8 %custom-call.32 = f32[1,128,128]{1,2,0:T(8,128)S(1)} custom-call(f32[1,128,128]{2,1,0:T(8,128)S(1)} %get-tuple-element.31), custom_call_target="InvertDiagBlocksLowerTriangular" | custom-call | tf_op jit(solution)/shard_map/jit(cholesky)/cholesky | solution.py:52
  212.0 1.2 convolution_subtract_fusion.4
  213.2 11.8 %cholesky.253 = f32[128,128]{1,0:T(8,128)S(1)} custom-call(f32[128,128]{1,0:T(8,128)S(1)} %convolution_subtract_fusion.4), custom_call_target="Cholesky" | custom-call | tf_op jit(solution)/shard_map/jit(cholesky)/cholesky | solution.py:52
  228.8 1.1 select_select_fusion
  229.9 13.6 %while.1 = (s32[]{:T(128)}, f32[512,512]{1,0:T(8,128)}, s32[4,2]{0,1:T(2,128)S(1)}, f32[4,128,128]{2,1,0:T(8,128)}, s32[]{:T(128)}) while((s32[]{:T(128)}, f32[512,512]{1,0:T(8,128)}, s32[4,2]{0,1:T(2,128)S(1)}, f32[4,128,128]{2,1,0:T(8,128)}, s32[]{:T(128)}) %tuple.39), condition=%wide.while_cond, body=%wide.while_body.sunk | while | flops 2 | bytes 132705 | solution.py:77
  230.6 2.8 bitcast_dynamic-update-slice_fusion.2
  234.0 2.8 bitcast_dynamic-update-slice_fusion.2
  237.4 2.8 bitcast_dynamic-update-slice_fusion.2
  240.8 2.7 bitcast_dynamic-update-slice_fusion.2
  243.6 40.1 %custom-call.33 = f32[4,128,128]{1,2,0:T(8,128)S(1)} custom-call(f32[4,128,128]{2,1,0:T(8,128)} %get-tuple-element.9), custom_call_target="InvertDiagBlocksLowerTriangular" | custom-call | tf_op jit(solution)/shard_map/triangular_solve | solution.py:77
  283.7 3.7 exponential_subtract_fusion
  288.5 1.9 convolution_subtract_fusion.1
  291.4 2.2 convolution_subtract_fusion
  294.7 3.0 fusion.9
  297.7 1.1 convolution_convert_fusion
  299.4 1.3 copy-done
  301.7 1.7 pad_maximum_fusion
  303.5 60.0 %all-reduce.4.cloned.1.call-done = f32[2560,256]{1,0:T(8,128)} async-done(((f32[2560,256]{1,0:T(8,128)}), f32[2560,256]{1,0:T(8,128)}) %all-reduce.4.cloned.1.call-update) | async-done | bytes 2621456 | tf_op jit(solution)/shard_map/psum | solution.py:98
  364.4 5.1 %multiply_reduce_fusion = f32[2048]{0:T(1024)S(1)} fusion(bf16[2048,2048]{1,0:T(8,128)(2,1)} %param.6), kind=kLoop, calls=%fused_computation.6 | loop fusion | flops 12580864 | bytes 8396800 | tf_op jit(solution)/shard_map/reduce_sum | solution.py:93
  369.5 10.5 %psum.30 = f32[2560]{0:T(1024)S(1)} all-reduce(f32[2560]{0:T(1024)S(1)} %pad_maximum_fusion.2), channel_id=1, replica_groups=mesh['row'=4,'col'=8] {'row'}, use_global_device_ids=true, to_apply=%region_18.19 | all-reduce | flops 2560 | bytes 20480 | tf_op jit(solution)/shard_map/psum | solution.py:98
  380.0 38.5 %psum.31 = f32[2560]{0:T(1024)S(1)} all-reduce(f32[2560]{0:T(1024)S(1)} %psum.30), channel_id=1, replica_groups=mesh['row'=4,'col'=8] {'col'}, use_global_device_ids=true, to_apply=%region_19.20 | all-reduce | flops 2560 | bytes 20480 | tf_op jit(solution)/shard_map/psum | solution.py:98
  418.5 65.2 %all-reduce.6.cloned.1.call-done = f32[2560,256]{1,0:T(8,128)} async-done(((f32[2560,256]{1,0:T(8,128)}), f32[2560,256]{1,0:T(8,128)}) %all-reduce.6.cloned.1.call-update) | async-done | bytes 2621456 | tf_op jit(solution)/shard_map/psum | solution.py:98
  483.8 2.1 divide_convert_fusion
  485.9 5.9 %convolution_bitcast_fusion = f32[2048,256]{0,1:T(8,128)S(1)} fusion(bf16[2048,2048]{1,0:T(8,128)(2,1)} %param.6, bf16[2560,256]{1,0:T(8,128)(2,1)S(1)} %divide_convert_fusion), kind=kOutput, calls=%fused_computation.21 | convolution fusion | flops 2147483648 | bytes 11534336 | tf_op jit(solution)/shard_map/dot_general | solution.py:101
  492.6 1.8 copy.24
  (79 shorter events, 17.3 us)
Async XLA Ops:
  7.2 51.6 %all-gather.6.cloned.1.call-start = ((), (), s32[]{:S(2)}) async-start(), calls=%async_computation.1 | async-start | bytes 1179648 | tf_op jit(solution)/shard_map/all_gather | solution.py:63
  14.5 61.2 %all-gather.4.cloned.1.call-start = ((), (), s32[]{:S(2)}) async-start(), calls=%async_computation | async-start | bytes 1310720 | tf_op jit(solution)/shard_map/all_gather | solution.py:66
  14.6 2.3 copy-start.2
  16.8 42.1 %copy-start.8 = (s32[32]{0:T(128)S(1)}, s32[32]{0:T(128)}, u32[]{:S(2)}) copy-start(s32[32]{0:T(128)} %param.9) | copy-start | bytes 388
  16.9 42.7 %copy-start.6 = (bf16[2048,256]{1,0:T(8,128)(2,1)S(1)}, bf16[2048,256]{1,0:T(8,128)(2,1)}, u32[]{:S(2)}) copy-start(bf16[2048,256]{1,0:T(8,128)(2,1)} %param.7) | copy-start | bytes 3145732
  53.1 58.6 %all-gather.8.cloned.1.call-start = ((), (), s32[]{:S(2)}) async-start(), calls=%async_computation.2 | async-start | bytes 5242880 | tf_op jit(solution)/shard_map/all_gather | solution.py:67
  58.8 304.7 %all-reduce.4.cloned.1.call-start = ((), (), s32[]{:S(2)}) async-start(), calls=%async_computation.3 | async-start | bytes 5242880 | tf_op jit(solution)/shard_map/psum | solution.py:98
  119.7 3.8 copy-start.4
  140.8 1.0 copy-start.3
  297.7 3.0 copy-start.7
  299.4 1.3 copy-start
  299.4 2.3 copy-start.5
  303.4 180.3 %all-reduce.6.cloned.1.call-start = ((), (), s32[]{:S(2)}) async-start(), calls=%async_computation.4 | async-start | bytes 5242880 | tf_op jit(solution)/shard_map/psum | solution.py:98
  485.9 5.9 %copy-start.1 = (bf16[512,2048]{1,0:T(8,128)(2,1)S(1)}, bf16[512,2048]{1,0:T(8,128)(2,1)}, u32[]{:S(2)}) copy-start(bf16[512,2048]{1,0:T(8,128)(2,1)} %copy-done) | copy-start | bytes 6291460
Sparse Core Ops, SparseCore 0:
  14.7 44.0 all-gather.5
  60.3 15.3 all-gather.3
  77.3 34.4 all-gather.7
  303.6 59.8 all-reduce.3
  367.0 116.6 all-reduce.5
